TPU v7x, 512 devices: a whole 4x4x16 slice. The times are simulated.
512 devices in a mesh: site: 16 (over z), fault: 32 (over x, y, core).
Axes of the slice: x: 4, y: 4, z: 16, core: 2. Of those that a mesh axis runs over, the one named last changes fastest.
Arguments:
- green_tensor: bfloat16 [16, 512, 96, 6, 256], P('site', 'fault'), may hold values from -0.375 to 0.375
- slip_map: bfloat16 [512, 8, 256], P('fault', None, 'site'), may hold values from 0.19921875 to 2
- rupture_time: float32 [512, 8, 256], P('fault', None, 'site'), may hold values from 0 to 48
- variation_ids: int32 [512, 8], P('fault'), may hold values from 0 to 7, each once within a row
- variation_count: int32 [512], P('fault'), may hold values from 2 to 8, as said below
- tile_rupture: int32 [512], P('fault'), may hold values from 0 to 31
- owner_slot: int32 [32], replicated, may hold values from 0 to 31, each once
Outputs:
- seismograms: float32 [32, 8, 16, 3, 192], P('fault', None, 'site')
Inputs may be any that keep to these rules, and one draw needn't show every extreme that they name: `variation_count`: every tile lists at least 2 of the 8 variations, and in every draw some tile lists all 8.
All inputs are finite; a program needn't handle non-finite values.
Results may differ from a plain program's by a relative error of at most 0.0027.
Values sent between devices are 32-bit elements; how exact they have to be, the bound alone decides.
No kernel may reach another device: no remote copies, remote signals or barrier semaphores. Data moves between devices by JAX's collectives and lax.ppermute only.
A program may use at most 64 MiB of HBM per device.

v0:
```python
import math

import jax
import jax.numpy as jnp
from jax import lax
from jax.sharding import PartitionSpec as P


def inverse_table(freq_count):
    sample_count = 2 * freq_count
    wave = jnp.arange(freq_count, dtype=jnp.int32)[:, None]
    sample = jnp.arange(sample_count, dtype=jnp.int32)[None, :]
    angles = 2.0 * math.pi / sample_count * (wave * sample % sample_count).astype(jnp.float32)
    return jnp.concatenate([jnp.cos(angles), -jnp.sin(angles)], axis=0) / math.sqrt(freq_count)


def tile_terms(amplitude, arrival, green_tile):
    freq_count = green_tile.shape[-3]
    frequency = jnp.arange(freq_count, dtype=jnp.float32)
    phases = (
        2.0 * math.pi / (2 * freq_count) * frequency[:, None, None] * jnp.expand_dims(arrival, -3)
    )
    amplitude_wide = jnp.expand_dims(amplitude, -3)
    a_real = (amplitude_wide * jnp.cos(phases)).astype(jnp.bfloat16)
    a_imag = (-amplitude_wide * jnp.sin(phases)).astype(jnp.bfloat16)
    part_real = jnp.einsum(
        "...fvp,...fkp->...vkf", a_real, green_tile, preferred_element_type=jnp.float32
    )
    part_imag = jnp.einsum(
        "...fvp,...fkp->...vkf", a_imag, green_tile, preferred_element_type=jnp.float32
    )
    flat_shape = part_real.shape[:-2] + (part_real.shape[-2] * part_real.shape[-1],)
    return jnp.stack([part_real.reshape(flat_shape), part_imag.reshape(flat_shape)], axis=-3)


def per_device(
    green_tensor, slip_map, rupture_time, variation_ids, variation_count, tile_rupture, owner_slot
):
    green_tiles = green_tensor[0]
    tile_total = green_tiles.shape[0]
    freq_count = green_tiles.shape[1]
    row_count = slip_map.shape[1]
    amplitude_local = slip_map.astype(jnp.float32)
    amplitude_piece = lax.all_gather(amplitude_local, "site", axis=2, tiled=True)
    arrival_piece = lax.all_gather(rupture_time, "site", axis=2, tiled=True)
    running = tile_terms(amplitude_piece, arrival_piece, green_tiles)
    split = running.reshape(tile_total, 2, row_count, 6, freq_count)
    real_part = split[:, 0, :, :3] - split[:, 1, :, 3:]
    imag_part = split[:, 0, :, 3:] + split[:, 1, :, :3]
    spectrum = jnp.concatenate([real_part, imag_part], axis=-1).reshape(tile_total, row_count, -1)
    is_live = jnp.arange(row_count, dtype=jnp.int32)[None, :] < variation_count[:, None]
    selector = (
        (variation_ids[:, None, :] == jnp.arange(row_count, dtype=jnp.int32)[None, :, None])
        & is_live[:, None, :]
    ).astype(jnp.float32)
    ordered = jnp.einsum("tvj,tjx->tvx", selector, spectrum, precision=lax.Precision.HIGHEST)
    rupture_total = owner_slot.shape[0]
    member = (tile_rupture[:, None] == jnp.arange(rupture_total, dtype=jnp.int32)[None, :]).astype(
        jnp.int32
    )
    slot_index = jnp.sum(member * owner_slot[None, :], axis=1)
    route = (slot_index[None, :] == jnp.arange(rupture_total, dtype=jnp.int32)[:, None]).astype(
        jnp.float32
    )
    local_sum = jnp.dot(
        route,
        ordered.reshape(tile_total, -1),
        precision=lax.Precision.HIGHEST,
        preferred_element_type=jnp.float32,
    )
    received = lax.all_to_all(local_sum, "fault", split_axis=0, concat_axis=0, tiled=True)
    devices = lax.axis_size("fault")
    owned_sum = jnp.sum(received.reshape(devices, rupture_total // devices, -1), axis=0)
    owned_rows = owned_sum.shape[0]
    table = inverse_table(freq_count)
    seismic = jnp.dot(
        owned_sum.reshape(-1, 2 * freq_count),
        table,
        precision=lax.Precision.HIGHEST,
        preferred_element_type=jnp.float32,
    )
    return seismic.reshape(owned_rows, row_count, 1, 3, 2 * freq_count)


def solution(mesh):
    placed = (
        P("site", "fault", None, None, None),
        P("fault", None, "site"),
        P("fault", None, "site"),
        P("fault", None),
        P("fault"),
        P("fault"),
        P(),
    )
    return jax.shard_map(
        per_device,
        mesh=mesh,
        in_specs=placed,
        out_specs=P("fault", None, "site", None, None),
        check_vma=False,
    )
```

profile of v0, /device:TPU:1, one launch (start us, length us, event | category | flops | bytes accessed | tf_op | source)
XLA Modules:
  0.0 200.4 jit_solution(4853131585115970853)
XLA Ops:
  0.0 0.9 copy.45
  0.9 35.4 %all_gather.6 = f32[16,8,256]{0,1,2:T(8,128)S(1)} all-gather(f32[16,8,16]{0,1,2:T(8,128)S(1)} %convert_element_type.17), channel_id=1, replica_groups=mesh['site'=16,'fault'=32] {'site'}, dimensions={2}, use_global_device_ids=true | all-gather | bytes 139264 | tf_op jit(solution)/shard_map/all_gather | solution.py:44
  36.3 0.4 copy.46
  36.7 0.9 copy.47
  37.7 25.2 %all_gather.7 = f32[16,8,256]{0,1,2:T(8,128)S(1)} all-gather(f32[16,8,16]{0,1,2:T(8,128)S(1)} %copy.47), channel_id=1, replica_groups=mesh['site'=16,'fault'=32] {'site'}, dimensions={2}, use_global_device_ids=true | all-gather | bytes 139264 | tf_op jit(solution)/shard_map/all_gather | solution.py:45
  62.9 0.4 copy.48
  63.3 43.4 %fusion.18 = f32[16,1,8,6,96]{2,3,4,0,1:T(8,128)S(1)} fusion(bf16[16,96,6,256]{3,1,2,0:T(8,128)(2,1)} %bitcast.24, f32[16,8,256]{2,1,0:T(8,128)S(1)} %copy.48, f32[96]{0:T(128)S(1)} %iota_multiply_fusion, f32[16,8,256]{2,1,0:T(8,128)S(1)} %copy.46), kind=kOutput, calls=%fused_computation.22 | convolution fusion | flops 47185920 | bytes 5276032 | tf_op jit(solution)/shard_map/...fvp,...fkp->...vkf/dot_general | solution.py:26
  106.7 43.9 %fusion.23 = f32[16,1,8,6,96]{2,3,4,0,1:T(8,128)S(1)} fusion(bf16[16,96,6,256]{3,1,2,0:T(8,128)(2,1)} %bitcast.25, f32[16,8,256]{2,1,0:T(8,128)S(1)} %neg.7, f32[16,8,256]{2,1,0:T(8,128)S(1)} %copy.48, f32[96]{0:T(128)S(1)} %iota_multiply_fusion), kind=kOutput, calls=%fused_computation.23 | convolution fusion | flops 47185920 | bytes 5276032 | tf_op jit(solution)/shard_map/...fvp,...fkp->...vkf/dot_general | solution.py:29
  150.5 1.7 fusion.17
  152.2 4.5 %pad_maximum_fusion = f32[16,8,3,192]{1,2,3,0:T(4,128)} fusion(f32[16,8,3,96]{1,2,3,0:T(4,128)S(1)} %get-tuple-element.6, f32[16,8,3,96]{1,2,3,0:T(4,128)S(1)} %get-tuple-element.5), kind=kLoop, calls=%fused_computation.10 | loop fusion | flops 73728 | bytes 589824 | tf_op jit(solution)/shard_map/concatenate | solution.py:50
  156.7 0.0 copy-start
  156.7 0.0 copy-start.1
  156.7 0.0 copy-start.2
  156.7 0.0 copy-start.3
  156.7 5.7 %copy.52 = f32[16,8,3,192]{3,2,1,0:T(4,128)S(1)} copy(f32[16,8,3,192]{1,2,3,0:T(4,128)} %pad_maximum_fusion) | data formatting | bytes 589824 | tf_op jit(solution)/shard_map/concatenate | solution.py:50
  162.4 0.3 reshape.58
  162.7 0.0 copy-done
  162.7 0.1 copy.44
  162.8 0.0 copy-done.1
  162.8 0.1 iota_compare_fusion.3
  162.9 0.3 fusion.40
  163.2 0.1 reshape.59
  163.3 0.0 copy-done.2
  163.3 0.0 copy-done.3
  163.3 0.2 select_reduce_fusion
  163.5 0.4 convolution_bitcast_fusion
  163.9 1.4 copy.53
  165.3 21.6 %all-to-all-start = ((f32[32,1,4608]{2,1,0:T(1,128)}), f32[32,1,4608]{2,1,0:T(1,128)S(1)}, u32[]{:S(2)}, u32[]{:S(2)}) async-start(f32[32,1,4608]{2,1,0:T(1,128)} %copy.53), calls=%async_computation | async-start | bytes 1179648 | tf_op jit(solution)/shard_map/all_to_all | solution.py:71
  186.9 0.4 sine_negate_fusion
  187.3 11.8 %all-to-all-done = f32[32,1,4608]{2,1,0:T(1,128)S(1)} async-done(((f32[32,1,4608]{2,1,0:T(1,128)}), f32[32,1,4608]{2,1,0:T(1,128)S(1)}, u32[]{:S(2)}, u32[]{:S(2)}) %all-to-all-start) | async-done | bytes 589856 | tf_op jit(solution)/shard_map/all_to_all | solution.py:71
  199.1 0.3 reduce_sum.19
  199.5 0.1 reshape.60
  199.6 0.2 convolution_bitcast_fusion.1
  199.8 0.6 copy.55
  (3 shorter events, 0.0 us)
Async XLA Ops:
  156.7 6.0 %copy-start = (s32[16,8]{0,1:T(8,128)S(1)}, s32[16,8]{0,1:T(8,128)}, u32[]{:S(2)}) copy-start(s32[16,8]{0,1:T(8,128)} %param.10) | copy-start | bytes 1540
  156.7 6.1 %copy-start.1 = (s32[16]{0:T(128)S(1)}, s32[16]{0:T(128)}, u32[]{:S(2)}) copy-start(s32[16]{0:T(128)} %param.11) | copy-start | bytes 196
  156.7 6.6 %copy-start.2 = (s32[32]{0:T(128)S(1)}, s32[32]{0:T(128)}, u32[]{:S(2)}) copy-start(s32[32]{0:T(128)} %param.13) | copy-start | bytes 388
  156.7 6.6 %copy-start.3 = (s32[16]{0:T(128)S(1)}, s32[16]{0:T(128)}, u32[]{:S(2)}) copy-start(s32[16]{0:T(128)} %param.12) | copy-start | bytes 196
  165.3 33.8 %all-to-all-start = ((f32[32,1,4608]{2,1,0:T(1,128)}), f32[32,1,4608]{2,1,0:T(1,128)S(1)}, u32[]{:S(2)}, u32[]{:S(2)}) async-start(f32[32,1,4608]{2,1,0:T(1,128)} %copy.53), calls=%async_computation | async-start | bytes 1179648 | tf_op jit(solution)/shard_map/all_to_all | solution.py:71
where the time goes:
time: 201 us; the launch traced here: 200 us
  matrix products  88.2 us (44%)
  blocking collectives  60.7 us (30%)
  starting transfers between devices  21.6 us (11%)
  waiting for transfers between devices  11.8 us (6%)
  local copies, waits for them, and re-layouts  10.8 us (5%)
  other arithmetic  7.19 us (4%)
    dot_general x1, matrix products, tile_terms(): jnp.einsum('...fvp,...fkp->...vkf', a_imag, green_tile, preferred_element...  43.9 us
    dot_general x1, matrix products, tile_terms(): jnp.einsum('...fvp,...fkp->...vkf', a_real, green_tile, preferred_element...  43.4 us
    all_gather x1, blocking collectives, per_device(): lax.all_gather(amplitude_local, 'site', axis=2, tiled=True)  35.4 us
    all_gather x1, blocking collectives, per_device(): arrival_piece = lax.all_gather(rupture_time, 'site', axis=2, tiled=True)  25.2 us
    all_to_all x1, starting transfers between devices, per_device(): lax.all_to_all(local_sum, 'fault', split_axis=0, concat_axis=0, tiled=True)  21.6 us
    all_to_all x1, waiting for transfers between devices, per_device(): lax.all_to_all(local_sum, 'fault', split_axis=0, concat_axis=0, tiled=True)  11.8 us
    concatenate x1, local copies, waits for them, and re-layouts, per_device(): jnp.concatenate([real_part, imag_part], axis=-1)  5.7 us
    concatenate x1, other arithmetic, per_device(): jnp.concatenate([real_part, imag_part], axis=-1)  4.47 us
  transfers between devices with their start and end apart: 1, of which 1 were waited for; matrix products, arithmetic and copies ran while one was open for 0% of the time, Pallas kernels for 0%

commit v1 on v0

v1 whole, which is shorter than its diff:
```python
import math

import jax
import jax.numpy as jnp
from jax import lax
from jax.experimental import pallas as pl
from jax.experimental.pallas import tpu as pltpu
from jax.sharding import PartitionSpec as P

STEP = 16


def sin_cos(angle):
    square = angle * angle
    sine = jnp.full_like(square, 1.0 / math.factorial(13))
    for order in (11, 9, 7, 5, 3, 1):
        sign = -1.0 if (order // 2) % 2 else 1.0
        sine = sine * square + sign / math.factorial(order)
    cosine = jnp.full_like(square, -1.0 / math.factorial(14))
    for order in (12, 10, 8, 6, 4, 2, 0):
        sign = -1.0 if (order // 2) % 2 else 1.0
        cosine = cosine * square + sign / math.factorial(order)
    return sine * angle, cosine


def turn(left, right):
    return (
        left[0] * right[0] - left[1] * right[1],
        left[0] * right[1] + left[1] * right[0],
    )


def pack_kernel(slip_hbm, time_hbm, out_ref, slip_ref, time_ref, sems):
    copies = [
        pltpu.make_async_copy(slip_hbm, slip_ref, sems.at[0]),
        pltpu.make_async_copy(time_hbm, time_ref, sems.at[1]),
    ]
    for copy in copies:
        copy.start()
    for copy in copies:
        copy.wait()
    slip = slip_ref[...].astype(jnp.float32).T
    arrival = time_ref[...].T
    block = jnp.concatenate([slip, arrival], axis=0)
    for peer in range(out_ref.shape[0]):
        out_ref[peer] = block


def main_kernel(maps_ref, key_ref, green_hbm, out_ref, green_ref, slip_ref, time_ref, spec_ref, sems):
    tiles, parts, freqs, points = green_ref.shape
    rows = slip_ref.shape[0] // tiles
    copies = [
        pltpu.make_async_copy(green_hbm.at[t], green_ref.at[t], sems.at[t]) for t in range(tiles)
    ]
    for copy in copies:
        copy.start()
    share = maps_ref.shape[1] // 2
    slip_ref[...] = maps_ref[:, :share, :].reshape(points, tiles * rows).T
    time_ref[...] = maps_ref[:, share:, :].reshape(points, tiles * rows).T
    chunks = freqs // STEP
    lanes = parts * STEP
    lane = lax.broadcasted_iota(jnp.int32, (2 * rows, lanes), 1) % STEP
    for t in range(tiles):
        angle = time_ref[t * rows : (t + 1) * rows, :] * (2.0 * math.pi / (2 * freqs))
        sine, cosine = sin_cos(angle)
        unit = (cosine, -sine)
        small = [None, unit]
        for b in range(2, STEP + 1):
            half = b // 2
            small.append(turn(small[half], small[b - half]))
        amplitude = slip_ref[t * rows : (t + 1) * rows, :]
        large = (amplitude, jnp.zeros_like(amplitude))
        copies[t].wait()
        for a in range(chunks):
            pieces = []
            for b in range(STEP):
                value = large if b == 0 else turn(large, small[b])
                pieces += [value[0], value[1]]
            phasor = jnp.concatenate(pieces, axis=0).astype(jnp.bfloat16)
            block = green_ref[t, :, a * STEP : (a + 1) * STEP, :].reshape(lanes, points)
            pairs = lax.dot_general(
                phasor, block, (((1,), (1,)), ((), ())), preferred_element_type=jnp.float32
            )
            own = pairs[: 2 * rows]
            for b in range(1, STEP):
                own = jnp.where(lane == b, pairs[b * 2 * rows : (b + 1) * 2 * rows], own)
            upper, lower = own[:rows], own[rows:]
            swapped = jnp.concatenate([-lower[:, lanes // 2 :], lower[:, : lanes // 2]], axis=1)
            spec_ref[t * rows : (t + 1) * rows, a * lanes : (a + 1) * lanes] = upper + swapped
            if a + 1 < chunks:
                large = turn(large, small[STEP])
    slots = out_ref.shape[0]
    chosen = lax.broadcasted_iota(jnp.int32, (slots, tiles * rows), 0) == key_ref[...]
    chosen = jnp.where(chosen, 1.0, 0.0).astype(jnp.bfloat16)
    spectrum = spec_ref[...]
    high = spectrum.astype(jnp.bfloat16)
    rest = spectrum - high.astype(jnp.float32)
    middle = rest.astype(jnp.bfloat16)
    low = (rest - middle.astype(jnp.float32)).astype(jnp.bfloat16)
    out_ref[...] = (
        jnp.dot(chosen, high, preferred_element_type=jnp.float32)
        + jnp.dot(chosen, middle, preferred_element_type=jnp.float32)
        + jnp.dot(chosen, low, preferred_element_type=jnp.float32)
    )


def final_kernel(received_ref, table_ref, out_ref):
    rows = received_ref.shape[1]
    width = received_ref.shape[2]
    total = jnp.sum(received_ref[...], axis=0)
    lanes = 6 * STEP
    chunks = width // lanes
    blocks = []
    for c in range(3):
        pieces = []
        for part in range(2):
            for a in range(chunks):
                first = a * lanes + (part * 3 + c) * STEP
                pieces.append(total[:, first : first + STEP])
        blocks.append(jnp.concatenate(pieces, axis=1))
    spectrum = jnp.concatenate(blocks, axis=0)
    out_ref[...] = jnp.dot(
        spectrum,
        table_ref[...],
        precision=lax.Precision.HIGHEST,
        preferred_element_type=jnp.float32,
    )


def inverse_table(freq_count):
    sample_count = 2 * freq_count
    wave = jnp.arange(freq_count, dtype=jnp.int32)[:, None]
    sample = jnp.arange(sample_count, dtype=jnp.int32)[None, :]
    angles = 2.0 * math.pi / sample_count * (wave * sample % sample_count).astype(jnp.float32)
    return jnp.concatenate([jnp.cos(angles), -jnp.sin(angles)], axis=0) / math.sqrt(freq_count)


def vmem():
    return pl.BlockSpec(memory_space=pltpu.VMEM)


def hbm():
    return pl.BlockSpec(memory_space=pltpu.HBM)


def in_hbm(array):
    return pltpu.with_memory_space_constraint(array, pltpu.HBM)


def per_device(
    green_tensor, slip_map, rupture_time, variation_ids, variation_count, tile_rupture, owner_slot
):
    _, tiles, freqs, parts, points = green_tensor.shape
    rows, share = slip_map.shape[1:]
    sites = points // share
    ruptures = owner_slot.shape[0]
    packed = pl.pallas_call(
        pack_kernel,
        in_specs=[hbm(), hbm()],
        out_specs=vmem(),
        out_shape=jax.ShapeDtypeStruct((sites, 2 * share, tiles * rows), jnp.float32),
        scratch_shapes=[
            pltpu.VMEM((tiles * rows, share), slip_map.dtype),
            pltpu.VMEM((tiles * rows, share), rupture_time.dtype),
            pltpu.SemaphoreType.DMA((2,)),
        ],
        compiler_params=pltpu.CompilerParams(vmem_limit_bytes=4 << 20),
        name="pack",
    )(in_hbm(slip_map.reshape(tiles * rows, share)), in_hbm(rupture_time.reshape(tiles * rows, share)))
    maps = lax.all_to_all(packed, "site", 0, 0, tiled=True)
    member = tile_rupture[:, None] == jnp.arange(ruptures, dtype=jnp.int32)[None, :]
    slot = jnp.sum(jnp.where(member, owner_slot[None, :], 0), axis=1)
    live = jnp.arange(rows, dtype=jnp.int32)[None, :] < variation_count[:, None]
    key = jnp.where(live, slot[:, None] * rows + variation_ids, -1).reshape(1, tiles * rows)
    green = jnp.transpose(green_tensor[0], (0, 2, 1, 3))
    partial = pl.pallas_call(
        main_kernel,
        in_specs=[vmem(), vmem(), hbm()],
        out_specs=vmem(),
        out_shape=jax.ShapeDtypeStruct((ruptures * rows, freqs * parts), jnp.float32),
        scratch_shapes=[
            pltpu.VMEM((tiles, parts, freqs, points), jnp.bfloat16),
            pltpu.VMEM((tiles * rows, points), jnp.float32),
            pltpu.VMEM((tiles * rows, points), jnp.float32),
            pltpu.VMEM((tiles * rows, freqs * parts), jnp.float32),
            pltpu.SemaphoreType.DMA((tiles,)),
        ],
        compiler_params=pltpu.CompilerParams(vmem_limit_bytes=16 << 20),
        name="spectra",
    )(maps, key, in_hbm(green))
    received = lax.all_to_all(
        partial.reshape(ruptures, rows, freqs * parts), "fault", 0, 0, tiled=True
    )
    seismic = pl.pallas_call(
        final_kernel,
        in_specs=[vmem(), vmem()],
        out_specs=vmem(),
        out_shape=jax.ShapeDtypeStruct((3 * rows, 2 * freqs), jnp.float32),
        compiler_params=pltpu.CompilerParams(vmem_limit_bytes=6 << 20),
        name="invert",
    )(received, inverse_table(freqs))
    seismic = seismic.reshape(3, rows, 2 * freqs).transpose(1, 0, 2)
    return seismic.reshape(1, rows, 1, 3, 2 * freqs)


def solution(mesh):
    placed = (
        P("site", "fault", None, None, None),
        P("fault", None, "site"),
        P("fault", None, "site"),
        P("fault", None),
        P("fault"),
        P("fault"),
        P(),
    )
    return jax.shard_map(
        per_device,
        mesh=mesh,
        in_specs=placed,
        out_specs=P("fault", None, "site", None, None),
        check_vma=False,
    )
```

time: 201 us -> 68.6 us (0.34)
  matrix products: 88.2 us -> 0 us
  blocking collectives: 60.7 us -> 0 us
  waiting for transfers between devices: 11.8 us -> 24.5 us
  Pallas kernels: 0 us -> 12.5 us
  local copies, waits for them, and re-layouts: 10.8 us -> 0.8 us
  starting transfers between devices: 21.6 us -> 28.4 us
  other arithmetic: 7.19 us -> 2 us
    dot_general x5 -> x0, matrix products: 88.2 us -> none  [the longest x1 43.9 us: tile_terms(): jnp.einsum('...fvp,...fkp->...vkf', a_imag, green_tile, preferred_element...]
    all_gather x2 -> x0, blocking collectives: 60.7 us -> none  [the longest x1 35.4 us: per_device(): lax.all_gather(amplitude_local, 'site', axis=2, tiled=True)]
    all_to_all x1 -> x2, waiting for transfers between devices: 11.8 us -> 24.5 us  [the longest x1 12.5 us: per_device(): lax.all_to_all(partial.reshape(ruptures, rows, freqs * parts), 'fault', 0...]
    pallas_call x0 -> x3, Pallas kernels: none -> 12.5 us  [the longest x1 10.5 us: per_device(): pl.pallas_call(main_kernel, in_specs=[vmem(), vmem(), hbm()], out_specs=v...]
    all_to_all x1 -> x2, starting transfers between devices: 21.6 us -> 28.4 us  [the longest x1 15.7 us: per_device(): maps = lax.all_to_all(packed, 'site', 0, 0, tiled=True)]
    concatenate x1 -> x0, local copies, waits for them, and re-layouts: 5.7 us -> none  [per_device(): jnp.concatenate([real_part, imag_part], axis=-1)]
    concatenate x1 -> x0, other arithmetic: 4.47 us -> none  [per_device(): jnp.concatenate([real_part, imag_part], axis=-1)]
  transfers between devices with their start and end apart: 1 -> 2, of which waited for: 1 -> 2; matrix products, arithmetic and copies ran while one was open for 0% -> 3% of each run, Pallas kernels for 0% -> 0%
where the time goes in v1:
time: 68.6 us; the launch traced here: 68.3 us
  starting transfers between devices  28.4 us (41%)
  waiting for transfers between devices  24.5 us (36%)
  Pallas kernels  12.5 us (18%)
  other arithmetic  2 us (3%)
  local copies, waits for them, and re-layouts  0.8 us (1%)
    all_to_all x1, starting transfers between devices, per_device(): maps = lax.all_to_all(packed, 'site', 0, 0, tiled=True)  15.7 us
    all_to_all x1, starting transfers between devices, per_device(): lax.all_to_all(partial.reshape(ruptures, rows, freqs * parts), 'fault', 0...  12.7 us
    all_to_all x1, waiting for transfers between devices, per_device(): lax.all_to_all(partial.reshape(ruptures, rows, freqs * parts), 'fault', 0...  12.5 us
    all_to_all x1, waiting for transfers between devices, per_device(): maps = lax.all_to_all(packed, 'site', 0, 0, tiled=True)  12.1 us
    pallas_call x1, Pallas kernels, per_device(): pl.pallas_call(main_kernel, in_specs=[vmem(), vmem(), hbm()], out_specs=v...  10.5 us
    pallas_call x1, Pallas kernels, per_device(): pl.pallas_call(pack_kernel, in_specs=[hbm(), hbm()], out_specs=vmem(), ou...  1.65 us
  transfers between devices with their start and end apart: 2, of which 2 were waited for; matrix products, arithmetic and copies ran while one was open for 3% of the time, Pallas kernels for 0%

profile of v1, /device:TPU:1, one launch (start us, length us, event | category | flops | bytes accessed | tf_op | source)
XLA Modules:
  0.0 68.3 jit_solution(1866371428947881088)
XLA Ops:
  0.0 1.7 %pack.1 = f32[16,32,128]{2,1,0:T(8,128)} custom-call(bf16[128,16]{1,0:T(8,128)(2,1)} %bitcast.14, f32[128,16]{1,0:T(8,128)} %bitcast.13), custom_call_target="tpu_custom_call" | custom-call | tf_op jit(solution)/shard_map/pack/pallas_call | solution.py:157
  1.7 15.7 %all-to-all-start = ((f32[16,32,128]{2,1,0:T(8,128)}), f32[16,32,128]{2,1,0:T(8,128)S(1)}, u32[]{:S(2)}, u32[]{:S(2)}) async-start(f32[16,32,128]{2,1,0:T(8,128)} %pack.1), calls=%async_computation | async-start | bytes 524288 | tf_op jit(solution)/shard_map/all_to_all | solution.py:170
  17.4 0.9 %select_reduce_fusion = s32[16]{0:T(128)S(1)} fusion(s32[32]{0:T(128)} %param.13, s32[16]{0:T(128)} %param.12), kind=kLoop, calls=%fused_computation.10 | loop fusion | flops 1520 | bytes 256 | tf_op jit(solution)/shard_map/reduce_sum | solution.py:172
  18.3 0.7 %add_select_fusion.1 = s32[16,8]{0,1:T(8,128)S(1)} fusion(s32[16,8]{0,1:T(8,128)} %param.10, s32[16]{0:T(128)S(1)} %broadcast_multiply_fusion, s32[16]{0:T(128)} %param.11), kind=kLoop, calls=%fused_computation.12 | loop fusion | flops 384 | bytes 1152 | tf_op jit(solution)/shard_map/jit(_where)/select_n | solution.py:174
  19.0 0.1 copy.12
  19.0 0.1 reshape.27.key_ref
  19.1 12.1 %all-to-all-done.maps_ref = f32[16,32,128]{2,1,0:T(8,128)S(1)} async-done(((f32[16,32,128]{2,1,0:T(8,128)}), f32[16,32,128]{2,1,0:T(8,128)S(1)}, u32[]{:S(2)}, u32[]{:S(2)}) %all-to-all-start) | async-done | bytes 262176 | tf_op jit(solution)/shard_map/all_to_all | solution.py:170
  31.2 10.5 %spectra.1 = f32[256,576]{1,0:T(8,128)} custom-call(f32[16,32,128]{2,1,0:T(8,128)S(1)} %all-to-all-done.maps_ref, s32[1,128]{1,0:T(1,128)S(1)} %reshape.27.key_ref, bf16[16,6,96,256]{3,2,1,0:T(8,128)(2,1)} %bitcast.12), custom_call_target="tpu_custom_call" | custom-call | tf_op jit(solution)/shard_map/spectra/pallas_call | solution.py:176
  41.7 12.7 %all-to-all-start.1 = ((f32[32,8,576]{2,1,0:T(8,128)}), f32[32,8,576]{2,1,0:T(8,128)S(1)}, u32[]{:S(2)}, u32[]{:S(2)}) async-start(f32[32,8,576]{2,1,0:T(8,128)} %bitcast.4), calls=%async_computation.1 | async-start | bytes 1310720 | tf_op jit(solution)/shard_map/all_to_all | solution.py:191
  54.4 0.4 sine_negate_fusion
  54.9 12.5 %all-to-all-done.1.received_ref = f32[32,8,576]{2,1,0:T(8,128)S(1)} async-done(((f32[32,8,576]{2,1,0:T(8,128)}), f32[32,8,576]{2,1,0:T(8,128)S(1)}, u32[]{:S(2)}, u32[]{:S(2)}) %all-to-all-start.1) | async-done | bytes 589856 | tf_op jit(solution)/shard_map/all_to_all | solution.py:191
  67.3 0.3 invert.1
  67.6 0.6 copy.13
  (2 shorter events, 0.0 us)
Async XLA Ops:
  1.7 29.5 %all-to-all-start = ((f32[16,32,128]{2,1,0:T(8,128)}), f32[16,32,128]{2,1,0:T(8,128)S(1)}, u32[]{:S(2)}, u32[]{:S(2)}) async-start(f32[16,32,128]{2,1,0:T(8,128)} %pack.1), calls=%async_computation | async-start | bytes 524288 | tf_op jit(solution)/shard_map/all_to_all | solution.py:170
  41.7 25.6 %all-to-all-start.1 = ((f32[32,8,576]{2,1,0:T(8,128)}), f32[32,8,576]{2,1,0:T(8,128)S(1)}, u32[]{:S(2)}, u32[]{:S(2)}) async-start(f32[32,8,576]{2,1,0:T(8,128)} %bitcast.4), calls=%async_computation.1 | async-start | bytes 1310720 | tf_op jit(solution)/shard_map/all_to_all | solution.py:191

commit v2 on v1

--- a/solution.py
+++ b/solution.py
@@ -8,6 +8,8 @@
 from jax.sharding import PartitionSpec as P
 
 STEP = 16
+AHEAD = 2
+GROUPS = (0, 2, 6)
 
 
 def sin_cos(angle):
@@ -30,23 +32,40 @@
     )
 
 
-def pack_kernel(slip_hbm, time_hbm, out_ref, slip_ref, time_ref, sems):
+def turn_both(left, right):
+    xx, yy = left[0] * right[0], left[1] * right[1]
+    xy, yx = left[0] * right[1], left[1] * right[0]
+    return (xx - yy, xy + yx), (xx + yy, yx - xy)
+
+
+def double(unit):
+    twice = unit[1] + unit[1]
+    return 1.0 - twice * unit[1], twice * unit[0]
+
+
+def pack_kernel(slip_hbm, time_hbm, out_hbm, slip_ref, time_ref, block_ref, sems):
     copies = [
         pltpu.make_async_copy(slip_hbm, slip_ref, sems.at[0]),
         pltpu.make_async_copy(time_hbm, time_ref, sems.at[1]),
     ]
     for copy in copies:
         copy.start()
-    for copy in copies:
-        copy.wait()
-    slip = slip_ref[...].astype(jnp.float32).T
-    arrival = time_ref[...].T
-    block = jnp.concatenate([slip, arrival], axis=0)
-    for peer in range(out_ref.shape[0]):
-        out_ref[peer] = block
-
-
-def main_kernel(maps_ref, key_ref, green_hbm, out_ref, green_ref, slip_ref, time_ref, spec_ref, sems):
+    share = slip_ref.shape[1]
+    copies[0].wait()
+    block_ref[:share] = slip_ref[...].astype(jnp.float32).T
+    copies[1].wait()
+    block_ref[share:] = time_ref[...].T
+    sends = [
+        pltpu.make_async_copy(block_ref, out_hbm.at[peer], sems.at[2 + peer])
+        for peer in range(out_hbm.shape[0])
+    ]
+    for send in sends:
+        send.start()
+    for send in sends:
+        send.wait()
+
+
+def main_kernel(maps_ref, key_ref, green_hbm, out_hbm, green_ref, slip_ref, time_ref, spec_ref, out_ref, sems):
     tiles, parts, freqs, points = green_ref.shape
     rows = slip_ref.shape[0] // tiles
     copies = [
@@ -58,24 +77,41 @@
     slip_ref[...] = maps_ref[:, :share, :].reshape(points, tiles * rows).T
     time_ref[...] = maps_ref[:, share:, :].reshape(points, tiles * rows).T
     chunks = freqs // STEP
+    middle = STEP // 2
     lanes = parts * STEP
     lane = lax.broadcasted_iota(jnp.int32, (2 * rows, lanes), 1) % STEP
-    for t in range(tiles):
+
+    def waves(t):
         angle = time_ref[t * rows : (t + 1) * rows, :] * (2.0 * math.pi / (2 * freqs))
         sine, cosine = sin_cos(angle)
-        unit = (cosine, -sine)
-        small = [None, unit]
-        for b in range(2, STEP + 1):
-            half = b // 2
-            small.append(turn(small[half], small[b - half]))
+        unit = {1: (cosine, -sine)}
+        unit[2] = double(unit[1])
+        unit[4] = double(unit[2])
+        unit[5], unit[3] = turn_both(unit[4], unit[1])
+        unit[6] = double(unit[3])
+        unit[7] = turn(unit[4], unit[3])
+        unit[8] = double(unit[4])
+        unit[16] = double(unit[8])
         amplitude = slip_ref[t * rows : (t + 1) * rows, :]
-        large = (amplitude, jnp.zeros_like(amplitude))
-        copies[t].wait()
+        return unit, (amplitude * unit[8][0], amplitude * unit[8][1])
+
+    ready = {t: waves(t) for t in range(min(AHEAD, tiles))}
+    for t in range(tiles):
+        if t in GROUPS:
+            last = min([g for g in GROUPS if g > t], default=tiles)
+            for copy in copies[t:last]:
+                copy.wait()
+        unit, center = ready.pop(t)
+        if t + AHEAD < tiles:
+            ready[t + AHEAD] = waves(t + AHEAD)
         for a in range(chunks):
+            values = {0: center}
+            for b in range(1, middle):
+                values[b], values[-b] = turn_both(center, unit[b])
+            values[-middle] = turn(center, (unit[middle][0], -unit[middle][1]))
             pieces = []
-            for b in range(STEP):
-                value = large if b == 0 else turn(large, small[b])
-                pieces += [value[0], value[1]]
+            for b in range(-middle, middle):
+                pieces += [values[b][0], values[b][1]]
             phasor = jnp.concatenate(pieces, axis=0).astype(jnp.bfloat16)
             block = green_ref[t, :, a * STEP : (a + 1) * STEP, :].reshape(lanes, points)
             pairs = lax.dot_general(
@@ -88,20 +124,26 @@
             swapped = jnp.concatenate([-lower[:, lanes // 2 :], lower[:, : lanes // 2]], axis=1)
             spec_ref[t * rows : (t + 1) * rows, a * lanes : (a + 1) * lanes] = upper + swapped
             if a + 1 < chunks:
-                large = turn(large, small[STEP])
+                center = turn(center, unit[STEP])
     slots = out_ref.shape[0]
     chosen = lax.broadcasted_iota(jnp.int32, (slots, tiles * rows), 0) == key_ref[...]
     chosen = jnp.where(chosen, 1.0, 0.0).astype(jnp.bfloat16)
+    chosen = jnp.concatenate([chosen, chosen], axis=1)
     spectrum = spec_ref[...]
     high = spectrum.astype(jnp.bfloat16)
-    rest = spectrum - high.astype(jnp.float32)
-    middle = rest.astype(jnp.bfloat16)
-    low = (rest - middle.astype(jnp.float32)).astype(jnp.bfloat16)
-    out_ref[...] = (
-        jnp.dot(chosen, high, preferred_element_type=jnp.float32)
-        + jnp.dot(chosen, middle, preferred_element_type=jnp.float32)
-        + jnp.dot(chosen, low, preferred_element_type=jnp.float32)
-    )
+    low = (spectrum - high.astype(jnp.float32)).astype(jnp.bfloat16)
+    both = jnp.concatenate([high, low], axis=0)
+    blocks = 4
+    size = slots // blocks
+    sends = []
+    for block in range(blocks):
+        part = slice(block * size, (block + 1) * size)
+        out_ref[part] = jnp.dot(chosen[part], both, preferred_element_type=jnp.float32)
+        send = pltpu.make_async_copy(out_ref.at[part], out_hbm.at[part], sems.at[tiles + block])
+        send.start()
+        sends.append(send)
+    for send in sends:
+        send.wait()
 
 
 def final_kernel(received_ref, table_ref, out_ref):
@@ -119,12 +161,15 @@
                 pieces.append(total[:, first : first + STEP])
         blocks.append(jnp.concatenate(pieces, axis=1))
     spectrum = jnp.concatenate(blocks, axis=0)
-    out_ref[...] = jnp.dot(
+    seismic = jnp.dot(
         spectrum,
         table_ref[...],
         precision=lax.Precision.HIGHEST,
         preferred_element_type=jnp.float32,
     )
+    for c in range(3):
+        for v in range(rows):
+            out_ref[v, c] = seismic[c * rows + v : c * rows + v + 1]
 
 
 def inverse_table(freq_count):
@@ -157,12 +202,13 @@
     packed = pl.pallas_call(
         pack_kernel,
         in_specs=[hbm(), hbm()],
-        out_specs=vmem(),
+        out_specs=hbm(),
         out_shape=jax.ShapeDtypeStruct((sites, 2 * share, tiles * rows), jnp.float32),
         scratch_shapes=[
             pltpu.VMEM((tiles * rows, share), slip_map.dtype),
             pltpu.VMEM((tiles * rows, share), rupture_time.dtype),
-            pltpu.SemaphoreType.DMA((2,)),
+            pltpu.VMEM((2 * share, tiles * rows), jnp.float32),
+            pltpu.SemaphoreType.DMA((2 + sites,)),
         ],
         compiler_params=pltpu.CompilerParams(vmem_limit_bytes=4 << 20),
         name="pack",
@@ -176,14 +222,15 @@
     partial = pl.pallas_call(
         main_kernel,
         in_specs=[vmem(), vmem(), hbm()],
-        out_specs=vmem(),
+        out_specs=hbm(),
         out_shape=jax.ShapeDtypeStruct((ruptures * rows, freqs * parts), jnp.float32),
         scratch_shapes=[
             pltpu.VMEM((tiles, parts, freqs, points), jnp.bfloat16),
             pltpu.VMEM((tiles * rows, points), jnp.float32),
             pltpu.VMEM((tiles * rows, points), jnp.float32),
             pltpu.VMEM((tiles * rows, freqs * parts), jnp.float32),
-            pltpu.SemaphoreType.DMA((tiles,)),
+            pltpu.VMEM((ruptures * rows, freqs * parts), jnp.float32),
+            pltpu.SemaphoreType.DMA((tiles + 4,)),
         ],
         compiler_params=pltpu.CompilerParams(vmem_limit_bytes=16 << 20),
         name="spectra",
@@ -195,12 +242,11 @@
         final_kernel,
         in_specs=[vmem(), vmem()],
         out_specs=vmem(),
-        out_shape=jax.ShapeDtypeStruct((3 * rows, 2 * freqs), jnp.float32),
+        out_shape=jax.ShapeDtypeStruct((rows, 3, 1, 2 * freqs), jnp.float32),
         compiler_params=pltpu.CompilerParams(vmem_limit_bytes=6 << 20),
         name="invert",
     )(received, inverse_table(freqs))
-    seismic = seismic.reshape(3, rows, 2 * freqs).transpose(1, 0, 2)
-    return seismic.reshape(1, rows, 1, 3, 2 * freqs)
+    return seismic.reshape(1, rows, 3, 1, 2 * freqs).transpose(0, 1, 3, 2, 4)
 
 
 def solution(mesh):

time: 68.6 us -> 64.8 us (0.945)
  Pallas kernels: 12.5 us -> 9.27 us
    pallas_call x2, Pallas kernels: 12.2 us -> 8.36 us  [the longest x1 6.58 us: per_device(): pl.pallas_call(main_kernel, in_specs=[vmem(), vmem(), hbm()], out_specs=h...]
where the time goes in v2:
time: 64.8 us; the launch traced here: 64.4 us
  starting transfers between devices  28.4 us (44%)
  waiting for transfers between devices  24.5 us (38%)
  Pallas kernels  9.27 us (14%)
  other arithmetic  2 us (3%)
    all_to_all x1, starting transfers between devices, per_device(): maps = lax.all_to_all(packed, 'site', 0, 0, tiled=True)  15.7 us
    all_to_all x1, starting transfers between devices, per_device(): lax.all_to_all(partial.reshape(ruptures, rows, freqs * parts), 'fault', 0...  12.7 us
    all_to_all x1, waiting for transfers between devices, per_device(): lax.all_to_all(partial.reshape(ruptures, rows, freqs * parts), 'fault', 0...  12.5 us
    all_to_all x1, waiting for transfers between devices, per_device(): maps = lax.all_to_all(packed, 'site', 0, 0, tiled=True)  12.1 us
    pallas_call x1, Pallas kernels, per_device(): pl.pallas_call(main_kernel, in_specs=[vmem(), vmem(), hbm()], out_specs=h...  6.58 us
    pallas_call x1, Pallas kernels, per_device(): pl.pallas_call(pack_kernel, in_specs=[hbm(), hbm()], out_specs=hbm(), out...  1.77 us
  transfers between devices with their start and end apart: 2, of which 2 were waited for; matrix products, arithmetic and copies ran while one was open for 3% of the time, Pallas kernels for 0%

profile of v2, /device:TPU:1, one launch (start us, length us, event | category | flops | bytes accessed | tf_op | source)
XLA Modules:
  0.0 64.4 jit_solution(3265643474318911473)
XLA Ops:
  0.0 1.8 %pack.1 = f32[16,32,128]{2,1,0:T(8,128)} custom-call(bf16[128,16]{1,0:T(8,128)(2,1)} %bitcast.11, f32[128,16]{1,0:T(8,128)} %bitcast.10), custom_call_target="tpu_custom_call" | custom-call | tf_op jit(solution)/shard_map/pack/pallas_call | solution.py:202
  1.8 15.7 %all-to-all-start = ((f32[16,32,128]{2,1,0:T(8,128)}), f32[16,32,128]{2,1,0:T(8,128)S(1)}, u32[]{:S(2)}, u32[]{:S(2)}) async-start(f32[16,32,128]{2,1,0:T(8,128)} %pack.1), calls=%async_computation | async-start | bytes 524288 | tf_op jit(solution)/shard_map/all_to_all | solution.py:216
  17.5 0.9 %select_reduce_fusion = s32[16]{0:T(128)S(1)} fusion(s32[32]{0:T(128)} %param.13, s32[16]{0:T(128)} %param.12), kind=kLoop, calls=%fused_computation.10 | loop fusion | flops 1520 | bytes 256 | tf_op jit(solution)/shard_map/reduce_sum | solution.py:218
  18.4 0.7 %add_select_fusion.1 = s32[16,8]{0,1:T(8,128)S(1)} fusion(s32[16,8]{0,1:T(8,128)} %param.10, s32[16]{0:T(128)S(1)} %broadcast_multiply_fusion, s32[16]{0:T(128)} %param.11), kind=kLoop, calls=%fused_computation.12 | loop fusion | flops 384 | bytes 1152 | tf_op jit(solution)/shard_map/jit(_where)/select_n | solution.py:220
  19.1 0.1 copy.12
  19.2 0.1 reshape.21.key_ref
  19.3 12.1 %all-to-all-done.maps_ref = f32[16,32,128]{2,1,0:T(8,128)S(1)} async-done(((f32[16,32,128]{2,1,0:T(8,128)}), f32[16,32,128]{2,1,0:T(8,128)S(1)}, u32[]{:S(2)}, u32[]{:S(2)}) %all-to-all-start) | async-done | bytes 262176 | tf_op jit(solution)/shard_map/all_to_all | solution.py:216
  31.3 6.6 %spectra.1 = f32[256,576]{1,0:T(8,128)} custom-call(f32[16,32,128]{2,1,0:T(8,128)S(1)} %all-to-all-done.maps_ref, s32[1,128]{1,0:T(1,128)S(1)} %reshape.21.key_ref, bf16[16,6,96,256]{3,2,1,0:T(8,128)(2,1)} %bitcast.9), custom_call_target="tpu_custom_call" | custom-call | tf_op jit(solution)/shard_map/spectra/pallas_call | solution.py:222
  37.9 12.7 %all-to-all-start.1 = ((f32[32,8,576]{2,1,0:T(8,128)}), f32[32,8,576]{2,1,0:T(8,128)S(1)}, u32[]{:S(2)}, u32[]{:S(2)}) async-start(f32[32,8,576]{2,1,0:T(8,128)} %bitcast.4), calls=%async_computation.1 | async-start | bytes 1310720 | tf_op jit(solution)/shard_map/all_to_all | solution.py:238
  50.6 0.4 sine_negate_fusion
  51.0 12.5 %all-to-all-done.1.received_ref = f32[32,8,576]{2,1,0:T(8,128)S(1)} async-done(((f32[32,8,576]{2,1,0:T(8,128)}), f32[32,8,576]{2,1,0:T(8,128)S(1)}, u32[]{:S(2)}, u32[]{:S(2)}) %all-to-all-start.1) | async-done | bytes 589856 | tf_op jit(solution)/shard_map/all_to_all | solution.py:238
  63.5 0.9 %invert.1 = f32[8,3,1,192]{3,2,1,0:T(1,128)} custom-call(f32[32,8,576]{2,1,0:T(8,128)S(1)} %all-to-all-done.1.received_ref, f32[192,192]{1,0:T(8,128)S(1)} %maximum_multiply_fusion.table_ref), custom_call_target="tpu_custom_call" | custom-call | tf_op jit(solution)/shard_map/invert/pallas_call | solution.py:241
  (2 shorter events, 0.0 us)
Async XLA Ops:
  1.8 29.5 %all-to-all-start = ((f32[16,32,128]{2,1,0:T(8,128)}), f32[16,32,128]{2,1,0:T(8,128)S(1)}, u32[]{:S(2)}, u32[]{:S(2)}) async-start(f32[16,32,128]{2,1,0:T(8,128)} %pack.1), calls=%async_computation | async-start | bytes 524288 | tf_op jit(solution)/shard_map/all_to_all | solution.py:216
  37.9 25.6 %all-to-all-start.1 = ((f32[32,8,576]{2,1,0:T(8,128)}), f32[32,8,576]{2,1,0:T(8,128)S(1)}, u32[]{:S(2)}, u32[]{:S(2)}) async-start(f32[32,8,576]{2,1,0:T(8,128)} %bitcast.4), calls=%async_computation.1 | async-start | bytes 1310720 | tf_op jit(solution)/shard_map/all_to_all | solution.py:238

commit v3 on v2

--- a/solution.py
+++ b/solution.py
@@ -9,7 +9,7 @@
 
 STEP = 16
 AHEAD = 2
-GROUPS = (0, 2, 6)
+EARLY = 6
 
 
 def sin_cos(angle):
@@ -65,13 +65,21 @@
         send.wait()
 
 
-def main_kernel(maps_ref, key_ref, green_hbm, out_hbm, green_ref, slip_ref, time_ref, spec_ref, out_ref, sems):
-    tiles, parts, freqs, points = green_ref.shape
+def load_kernel(green_hbm, green_ref, sem):
+    copy = pltpu.make_async_copy(green_hbm.at[: green_ref.shape[0]], green_ref, sem)
+    copy.start()
+    copy.wait()
+
+
+def main_kernel(maps_ref, key_ref, first_ref, green_hbm, out_ref, green_ref, slip_ref, time_ref, spec_ref, sems):
+    tiles, parts, freqs, points = green_hbm.shape
+    early = first_ref.shape[0]
     rows = slip_ref.shape[0] // tiles
-    copies = [
-        pltpu.make_async_copy(green_hbm.at[t], green_ref.at[t], sems.at[t]) for t in range(tiles)
-    ]
-    for copy in copies:
+    copies = {
+        t: pltpu.make_async_copy(green_hbm.at[t], green_ref.at[t - early], sems.at[t - early])
+        for t in range(early, tiles)
+    }
+    for copy in copies.values():
         copy.start()
     share = maps_ref.shape[1] // 2
     slip_ref[...] = maps_ref[:, :share, :].reshape(points, tiles * rows).T
@@ -95,12 +103,17 @@
         amplitude = slip_ref[t * rows : (t + 1) * rows, :]
         return unit, (amplitude * unit[8][0], amplitude * unit[8][1])
 
+    def keep():
+        for t, a in list(done):
+            spec_ref[t * rows : (t + 1) * rows, a * lanes : (a + 1) * lanes] = done.pop((t, a))
+
+    done = {}
     ready = {t: waves(t) for t in range(min(AHEAD, tiles))}
     for t in range(tiles):
-        if t in GROUPS:
-            last = min([g for g in GROUPS if g > t], default=tiles)
-            for copy in copies[t:last]:
+        if t == early:
+            for copy in copies.values():
                 copy.wait()
+        keep()
         unit, center = ready.pop(t)
         if t + AHEAD < tiles:
             ready[t + AHEAD] = waves(t + AHEAD)
@@ -113,7 +126,8 @@
             for b in range(-middle, middle):
                 pieces += [values[b][0], values[b][1]]
             phasor = jnp.concatenate(pieces, axis=0).astype(jnp.bfloat16)
-            block = green_ref[t, :, a * STEP : (a + 1) * STEP, :].reshape(lanes, points)
+            source = first_ref.at[t] if t < early else green_ref.at[t - early]
+            block = source[:, a * STEP : (a + 1) * STEP, :].reshape(lanes, points)
             pairs = lax.dot_general(
                 phasor, block, (((1,), (1,)), ((), ())), preferred_element_type=jnp.float32
             )
@@ -122,28 +136,21 @@
                 own = jnp.where(lane == b, pairs[b * 2 * rows : (b + 1) * 2 * rows], own)
             upper, lower = own[:rows], own[rows:]
             swapped = jnp.concatenate([-lower[:, lanes // 2 :], lower[:, : lanes // 2]], axis=1)
-            spec_ref[t * rows : (t + 1) * rows, a * lanes : (a + 1) * lanes] = upper + swapped
+            done[t, a] = upper + swapped
             if a + 1 < chunks:
                 center = turn(center, unit[STEP])
-    slots = out_ref.shape[0]
+    keep()
+    slots, width = out_ref.shape
     chosen = lax.broadcasted_iota(jnp.int32, (slots, tiles * rows), 0) == key_ref[...]
     chosen = jnp.where(chosen, 1.0, 0.0).astype(jnp.bfloat16)
     chosen = jnp.concatenate([chosen, chosen], axis=1)
-    spectrum = spec_ref[...]
-    high = spectrum.astype(jnp.bfloat16)
-    low = (spectrum - high.astype(jnp.float32)).astype(jnp.bfloat16)
-    both = jnp.concatenate([high, low], axis=0)
-    blocks = 4
-    size = slots // blocks
-    sends = []
-    for block in range(blocks):
-        part = slice(block * size, (block + 1) * size)
-        out_ref[part] = jnp.dot(chosen[part], both, preferred_element_type=jnp.float32)
-        send = pltpu.make_async_copy(out_ref.at[part], out_hbm.at[part], sems.at[tiles + block])
-        send.start()
-        sends.append(send)
-    for send in sends:
-        send.wait()
+    for first in range(0, width, 256):
+        part = slice(first, min(first + 256, width))
+        spectrum = spec_ref[:, part]
+        high = spectrum.astype(jnp.bfloat16)
+        low = (spectrum - high.astype(jnp.float32)).astype(jnp.bfloat16)
+        both = jnp.concatenate([high, low], axis=0)
+        out_ref[:, part] = jnp.dot(chosen, both, preferred_element_type=jnp.float32)
 
 
 def final_kernel(received_ref, table_ref, out_ref):
@@ -218,23 +225,33 @@
     slot = jnp.sum(jnp.where(member, owner_slot[None, :], 0), axis=1)
     live = jnp.arange(rows, dtype=jnp.int32)[None, :] < variation_count[:, None]
     key = jnp.where(live, slot[:, None] * rows + variation_ids, -1).reshape(1, tiles * rows)
-    green = jnp.transpose(green_tensor[0], (0, 2, 1, 3))
+    green = in_hbm(jnp.transpose(green_tensor[0], (0, 2, 1, 3)))
+    early = min(EARLY, tiles // 2)
+    first = pl.pallas_call(
+        load_kernel,
+        in_specs=[hbm()],
+        out_specs=vmem(),
+        out_shape=jax.ShapeDtypeStruct((early, *green.shape[1:]), green.dtype),
+        scratch_shapes=[pltpu.SemaphoreType.DMA(())],
+        compiler_params=pltpu.CompilerParams(vmem_limit_bytes=4 << 20),
+        name="load",
+    )(green)
     partial = pl.pallas_call(
         main_kernel,
-        in_specs=[vmem(), vmem(), hbm()],
-        out_specs=hbm(),
+        in_specs=[vmem(), vmem(), vmem(), hbm()],
+        out_specs=vmem(),
         out_shape=jax.ShapeDtypeStruct((ruptures * rows, freqs * parts), jnp.float32),
         scratch_shapes=[
-            pltpu.VMEM((tiles, parts, freqs, points), jnp.bfloat16),
+            pltpu.VMEM((tiles - early, parts, freqs, points), jnp.bfloat16),
             pltpu.VMEM((tiles * rows, points), jnp.float32),
             pltpu.VMEM((tiles * rows, points), jnp.float32),
             pltpu.VMEM((tiles * rows, freqs * parts), jnp.float32),
-            pltpu.VMEM((ruptures * rows, freqs * parts), jnp.float32),
-            pltpu.SemaphoreType.DMA((tiles + 4,)),
+            pltpu.SemaphoreType.DMA((tiles - early,)),
         ],
         compiler_params=pltpu.CompilerParams(vmem_limit_bytes=16 << 20),
         name="spectra",
-    )(maps, key, in_hbm(green))
+    )(maps, key, first, green)
+    partial, table = lax.optimization_barrier((partial, inverse_table(freqs)))
     received = lax.all_to_all(
         partial.reshape(ruptures, rows, freqs * parts), "fault", 0, 0, tiled=True
     )
@@ -245,7 +262,7 @@
         out_shape=jax.ShapeDtypeStruct((rows, 3, 1, 2 * freqs), jnp.float32),
         compiler_params=pltpu.CompilerParams(vmem_limit_bytes=6 << 20),
         name="invert",
-    )(received, inverse_table(freqs))
+    )(received, table)
     return seismic.reshape(1, rows, 3, 1, 2 * freqs).transpose(0, 1, 3, 2, 4)
 
 

time: 64.8 us -> 63.6 us (0.981)
  blocking collectives: 0 us -> 25.4 us
  waiting for transfers between devices: 24.5 us -> 11.4 us
  starting transfers between devices: 28.4 us -> 15.7 us
  other arithmetic: 2 us -> 0.64 us
    all_to_all x0 -> x1, blocking collectives: none -> 25.4 us  [per_device(): lax.all_to_all(partial.reshape(ruptures, rows, freqs * parts), 'fault', 0...]
    all_to_all x1 -> x0, starting transfers between devices: 12.7 us -> none  [per_device(): lax.all_to_all(partial.reshape(ruptures, rows, freqs * parts), 'fault', 0...]
    all_to_all x1 -> x0, waiting for transfers between devices: 12.5 us -> none  [per_device(): lax.all_to_all(partial.reshape(ruptures, rows, freqs * parts), 'fault', 0...]
    select_n x1, other arithmetic: 0.7 us -> 0.01 us  [per_device(): jnp.where(live, slot[:, None] * rows + variation_ids, -1)]
    reduce_sum x1, other arithmetic: 0.85 us -> 0.18 us  [per_device(): slot = jnp.sum(jnp.where(member, owner_slot[None, :], 0), axis=1)]
    pallas_call x1 -> x2, Pallas kernels: 6.58 us -> 7.15 us  [the longest x1 5.66 us: per_device(): pl.pallas_call(main_kernel, in_specs=[vmem(), vmem(), vmem(), hbm()], out...]
  transfers between devices with their start and end apart: 2 -> 1, of which waited for: 2 -> 1; matrix products, arithmetic and copies ran while one was open for 3% -> 1% of each run, Pallas kernels for 0% -> 2%
where the time goes in v3:
time: 63.6 us; the launch traced here: 63.3 us
  blocking collectives  25.4 us (40%)
  starting transfers between devices  15.7 us (25%)
  waiting for transfers between devices  11.4 us (18%)
  Pallas kernels  9.88 us (16%)
  other arithmetic  0.64 us (1%)
    all_to_all x1, blocking collectives, per_device(): lax.all_to_all(partial.reshape(ruptures, rows, freqs * parts), 'fault', 0...  25.4 us
    all_to_all x1, starting transfers between devices, per_device(): maps = lax.all_to_all(packed, 'site', 0, 0, tiled=True)  15.7 us
    all_to_all x1, waiting for transfers between devices, per_device(): maps = lax.all_to_all(packed, 'site', 0, 0, tiled=True)  11.4 us
    pallas_call x1, Pallas kernels, per_device(): pl.pallas_call(main_kernel, in_specs=[vmem(), vmem(), vmem(), hbm()], out...  5.66 us
    pallas_call x1, Pallas kernels, per_device(): pl.pallas_call(pack_kernel, in_specs=[hbm(), hbm()], out_specs=hbm(), out...  1.82 us
    pallas_call x1, Pallas kernels, per_device(): pl.pallas_call(load_kernel, in_specs=[hbm()], out_specs=vmem(), out_shape...  1.49 us
  transfers between devices with their start and end apart: 1, of which 1 were waited for; matrix products, arithmetic and copies ran while one was open for 1% of the time, Pallas kernels for 2%

profile of v3, /device:TPU:1, one launch (start us, length us, event | category | flops | bytes accessed | tf_op | source)
XLA Modules:
  0.0 63.3 jit_solution(5608956155278957186)
XLA Ops:
  0.0 0.0 copy-start.3
  0.0 0.0 copy-start.2
  0.0 0.0 copy-start
  0.0 0.0 copy-start.1
  0.0 1.8 %pack.1 = f32[16,32,128]{2,1,0:T(8,128)} custom-call(bf16[128,16]{1,0:T(8,128)(2,1)} %bitcast.13, f32[128,16]{1,0:T(8,128)} %bitcast.12), custom_call_target="tpu_custom_call" | custom-call | tf_op jit(solution)/shard_map/pack/pallas_call | solution.py:209
  1.9 15.7 %all-to-all-start = ((f32[16,32,128]{2,1,0:T(8,128)}), f32[16,32,128]{2,1,0:T(8,128)S(1)}, u32[]{:S(2)}, u32[]{:S(2)}) async-start(f32[16,32,128]{2,1,0:T(8,128)} %pack.1), calls=%async_computation | async-start | bytes 524288 | tf_op jit(solution)/shard_map/all_to_all | solution.py:223
  17.6 1.5 %load.1.first_ref = bf16[6,6,96,256]{3,2,1,0:T(8,128)(2,1)S(1)} custom-call(bf16[16,6,96,256]{3,2,1,0:T(8,128)(2,1)} %bitcast.10), custom_call_target="tpu_custom_call" | custom-call | tf_op jit(solution)/shard_map/load/pallas_call | solution.py:230
  19.1 0.0 copy-done.3
  19.1 0.0 copy-done.2
  19.1 0.2 select_reduce_fusion
  19.3 0.0 copy-done
  19.3 0.0 copy-done.1
  19.3 0.1 copy.12
  19.4 0.1 reshape.21.key_ref
  19.5 0.4 sine_negate_fusion
  20.0 11.4 %all-to-all-done.maps_ref = f32[16,32,128]{2,1,0:T(8,128)S(1)} async-done(((f32[16,32,128]{2,1,0:T(8,128)}), f32[16,32,128]{2,1,0:T(8,128)S(1)}, u32[]{:S(2)}, u32[]{:S(2)}) %all-to-all-start) | async-done | bytes 262176 | tf_op jit(solution)/shard_map/all_to_all | solution.py:223
  31.4 5.7 %spectra.1 = f32[256,576]{1,0:T(8,128)S(1)} custom-call(f32[16,32,128]{2,1,0:T(8,128)S(1)} %all-to-all-done.maps_ref, s32[1,128]{1,0:T(1,128)S(1)} %reshape.21.key_ref, bf16[6,6,96,256]{3,2,1,0:T(8,128)(2,1)S(1)} %load.1.first_ref, bf16[16,6,96,256]{3,2,1,0:T(8,128)(2,1)} %bitcast.11), custom_call_target="tpu_custom_call" | custom-call | tf_op jit(solution)/shard_map/spectra/pallas_call | solution.py:239
  37.0 25.4 %all_to_all.10.received_ref = f32[32,8,576]{2,1,0:T(8,128)S(1)} all-to-all(f32[32,8,576]{2,1,0:T(8,128)S(1)} %bitcast.9), channel_id=1, replica_groups=mesh['site'=16,'fault'=32] {'fault'}, dimensions={0} | all-to-all | bytes 1179648 | tf_op jit(solution)/shard_map/all_to_all | solution.py:255
  62.4 0.9 %invert.1 = f32[8,3,1,192]{3,2,1,0:T(1,128)} custom-call(f32[32,8,576]{2,1,0:T(8,128)S(1)} %all_to_all.10.received_ref, f32[192,192]{1,0:T(8,128)S(1)} %maximum_multiply_fusion.table_ref), custom_call_target="tpu_custom_call" | custom-call | tf_op jit(solution)/shard_map/invert/pallas_call | solution.py:258
  (3 shorter events, 0.0 us)
Async XLA Ops:
  0.0 19.1 %copy-start.3 = (s32[16]{0:T(128)S(1)}, s32[16]{0:T(128)}, u32[]{:S(2)}) copy-start(s32[16]{0:T(128)} %param.12) | copy-start | bytes 196
  0.0 19.1 %copy-start.2 = (s32[32]{0:T(128)S(1)}, s32[32]{0:T(128)}, u32[]{:S(2)}) copy-start(s32[32]{0:T(128)} %param.13) | copy-start | bytes 388
  0.0 19.3 %copy-start = (s32[16,8]{0,1:T(8,128)S(1)}, s32[16,8]{0,1:T(8,128)}, u32[]{:S(2)}) copy-start(s32[16,8]{0,1:T(8,128)} %param.10) | copy-start | bytes 1540
  0.0 19.3 %copy-start.1 = (s32[16]{0:T(128)S(1)}, s32[16]{0:T(128)}, u32[]{:S(2)}) copy-start(s32[16]{0:T(128)} %param.11) | copy-start | bytes 196
  1.9 29.5 %all-to-all-start = ((f32[16,32,128]{2,1,0:T(8,128)}), f32[16,32,128]{2,1,0:T(8,128)S(1)}, u32[]{:S(2)}, u32[]{:S(2)}) async-start(f32[16,32,128]{2,1,0:T(8,128)} %pack.1), calls=%async_computation | async-start | bytes 524288 | tf_op jit(solution)/shard_map/all_to_all | solution.py:223

commit v4 on v3

--- a/solution.py
+++ b/solution.py
@@ -41,6 +41,12 @@
 def double(unit):
     twice = unit[1] + unit[1]
     return 1.0 - twice * unit[1], twice * unit[0]
+
+
+def two_terms(value):
+    high = value.astype(jnp.bfloat16)
+    low = (value - high.astype(jnp.float32)).astype(jnp.bfloat16)
+    return jnp.concatenate([high, low], axis=0)
 
 
 def pack_kernel(slip_hbm, time_hbm, out_hbm, slip_ref, time_ref, block_ref, sems):
@@ -140,23 +146,60 @@
             if a + 1 < chunks:
                 center = turn(center, unit[STEP])
     keep()
-    slots, width = out_ref.shape
-    chosen = lax.broadcasted_iota(jnp.int32, (slots, tiles * rows), 0) == key_ref[...]
-    chosen = jnp.where(chosen, 1.0, 0.0).astype(jnp.bfloat16)
+    width = spec_ref.shape[1]
+    slots = out_ref.shape[0] * 128 // (rows * width)
+    height = rows * width // 128
+    half = rows // 2
+    row = lax.broadcasted_iota(jnp.int32, (slots * rows, tiles * rows), 0)
+    turned = row // rows * rows + (row % rows + (row // rows) % 2 * half) % rows
+    key = key_ref[...]
+    chosen = jnp.where(turned == key, 1.0, 0.0).astype(jnp.bfloat16)
     chosen = jnp.concatenate([chosen, chosen], axis=1)
-    for first in range(0, width, 256):
-        part = slice(first, min(first + 256, width))
-        spectrum = spec_ref[:, part]
-        high = spectrum.astype(jnp.bfloat16)
-        low = (spectrum - high.astype(jnp.float32)).astype(jnp.bfloat16)
-        both = jnp.concatenate([high, low], axis=0)
-        out_ref[:, part] = jnp.dot(chosen, both, preferred_element_type=jnp.float32)
+    whole = width // 128 * 128
+    for first in range(0, whole, 256):
+        both = two_terms(spec_ref[:, first : first + 256])
+        routed = jnp.dot(chosen, both, preferred_element_type=jnp.float32)
+        for slot in range(slots):
+            for block in range(2):
+                base = slot * height + (first // 128 + block) * rows
+                piece = routed[slot * rows : (slot + 1) * rows, block * 128 : (block + 1) * 128]
+                if slot % 2:
+                    out_ref[base : base + half] = piece[half:]
+                    out_ref[base + half : base + rows] = piece[:half]
+                else:
+                    out_ref[base : base + rows] = piece
+    row = lax.broadcasted_iota(jnp.int32, (slots * half, tiles * rows), 0)
+    lower = row // half * rows + row % half
+    left = jnp.where(lower == key, 1.0, 0.0).astype(jnp.bfloat16)
+    right = jnp.where(lower + half == key, 1.0, 0.0).astype(jnp.bfloat16)
+    both = two_terms(spec_ref[:, whole:])
+    blank = jnp.zeros_like(both)
+    routed = jnp.dot(
+        jnp.concatenate([left, left], axis=1),
+        jnp.concatenate([both, blank], axis=1),
+        preferred_element_type=jnp.float32,
+    ) + jnp.dot(
+        jnp.concatenate([right, right], axis=1),
+        jnp.concatenate([blank, both], axis=1),
+        preferred_element_type=jnp.float32,
+    )
+    for slot in range(slots):
+        base = slot * height + height - half
+        out_ref[base : base + half] = routed[slot * half : (slot + 1) * half]
 
 
 def final_kernel(received_ref, table_ref, out_ref):
-    rows = received_ref.shape[1]
-    width = received_ref.shape[2]
-    total = jnp.sum(received_ref[...], axis=0)
+    rows = out_ref.shape[0]
+    width = 3 * table_ref.shape[0]
+    height = rows * width // 128
+    pairs = received_ref[: 2 * height]
+    for source in range(1, received_ref.shape[0] // (2 * height)):
+        pairs += received_ref[source * 2 * height : (source + 1) * 2 * height]
+    summed = pairs[:height] + pairs[height:]
+    pieces = [summed[first : first + rows] for first in range(0, height - rows // 2, rows)]
+    last = summed[height - rows // 2 :]
+    pieces.append(jnp.concatenate([last[:, :64], last[:, 64:]], axis=0))
+    total = jnp.concatenate(pieces, axis=1)
     lanes = 6 * STEP
     chunks = width // lanes
     blocks = []
@@ -240,7 +283,7 @@
         main_kernel,
         in_specs=[vmem(), vmem(), vmem(), hbm()],
         out_specs=vmem(),
-        out_shape=jax.ShapeDtypeStruct((ruptures * rows, freqs * parts), jnp.float32),
+        out_shape=jax.ShapeDtypeStruct((ruptures * rows * freqs * parts // 128, 128), jnp.float32),
         scratch_shapes=[
             pltpu.VMEM((tiles - early, parts, freqs, points), jnp.bfloat16),
             pltpu.VMEM((tiles * rows, points), jnp.float32),
@@ -253,8 +296,8 @@
     )(maps, key, first, green)
     partial, table = lax.optimization_barrier((partial, inverse_table(freqs)))
     received = lax.all_to_all(
-        partial.reshape(ruptures, rows, freqs * parts), "fault", 0, 0, tiled=True
-    )
+        partial.reshape(ruptures, -1, rows // 2, 128), "fault", 0, 0, tiled=True
+    ).reshape(-1, 128)
     seismic = pl.pallas_call(
         final_kernel,
         in_specs=[vmem(), vmem()],

time: 63.6 us -> 63 us (level)
  blocking collectives: 25.4 us -> 24.7 us
    all_to_all x1, blocking collectives: 25.4 us -> 24.7 us  [per_device(): lax.all_to_all(partial.reshape(ruptures, -1, rows // 2, 128), 'fault', 0,...]
where the time goes in v4:
time: 63 us; the launch traced here: 62.7 us
  blocking collectives  24.7 us (39%)
  starting transfers between devices  15.7 us (25%)
  waiting for transfers between devices  11.4 us (18%)
  Pallas kernels  9.89 us (16%)
  other arithmetic  0.64 us (1%)
    all_to_all x1, blocking collectives, per_device(): lax.all_to_all(partial.reshape(ruptures, -1, rows // 2, 128), 'fault', 0,...  24.7 us
    all_to_all x1, starting transfers between devices, per_device(): maps = lax.all_to_all(packed, 'site', 0, 0, tiled=True)  15.7 us
    all_to_all x1, waiting for transfers between devices, per_device(): maps = lax.all_to_all(packed, 'site', 0, 0, tiled=True)  11.4 us
    pallas_call x1, Pallas kernels, per_device(): pl.pallas_call(main_kernel, in_specs=[vmem(), vmem(), vmem(), hbm()], out...  5.63 us
    pallas_call x1, Pallas kernels, per_device(): pl.pallas_call(pack_kernel, in_specs=[hbm(), hbm()], out_specs=hbm(), out...  1.82 us
    pallas_call x1, Pallas kernels, per_device(): pl.pallas_call(load_kernel, in_specs=[hbm()], out_specs=vmem(), out_shape...  1.49 us
  transfers between devices with their start and end apart: 1, of which 1 were waited for; matrix products, arithmetic and copies ran while one was open for 1% of the time, Pallas kernels for 2%

profile of v4, /device:TPU:1, one launch (start us, length us, event | category | flops | bytes accessed | tf_op | source)
XLA Modules:
  0.0 62.7 jit_solution(29044876116520196)
XLA Ops:
  0.0 0.0 copy-start.3
  0.0 0.0 copy-start.2
  0.0 0.0 copy-start
  0.0 0.0 copy-start.1
  0.0 1.8 %pack.1 = f32[16,32,128]{2,1,0:T(8,128)} custom-call(bf16[128,16]{1,0:T(8,128)(2,1)} %bitcast.15, f32[128,16]{1,0:T(8,128)} %bitcast.14), custom_call_target="tpu_custom_call" | custom-call | tf_op jit(solution)/shard_map/pack/pallas_call | solution.py:252
  1.9 15.7 %all-to-all-start = ((f32[16,32,128]{2,1,0:T(8,128)}), f32[16,32,128]{2,1,0:T(8,128)S(1)}, u32[]{:S(2)}, u32[]{:S(2)}) async-start(f32[16,32,128]{2,1,0:T(8,128)} %pack.1), calls=%async_computation | async-start | bytes 524288 | tf_op jit(solution)/shard_map/all_to_all | solution.py:266
  17.6 1.5 %load.1.first_ref = bf16[6,6,96,256]{3,2,1,0:T(8,128)(2,1)S(1)} custom-call(bf16[16,6,96,256]{3,2,1,0:T(8,128)(2,1)} %bitcast.12), custom_call_target="tpu_custom_call" | custom-call | tf_op jit(solution)/shard_map/load/pallas_call | solution.py:273
  19.1 0.0 copy-done.3
  19.1 0.0 copy-done.2
  19.1 0.2 select_reduce_fusion
  19.3 0.0 copy-done
  19.3 0.0 copy-done.1
  19.3 0.1 copy.12
  19.4 0.1 reshape.24.key_ref
  19.5 0.4 sine_negate_fusion
  20.0 11.4 %all-to-all-done.maps_ref = f32[16,32,128]{2,1,0:T(8,128)S(1)} async-done(((f32[16,32,128]{2,1,0:T(8,128)}), f32[16,32,128]{2,1,0:T(8,128)S(1)}, u32[]{:S(2)}, u32[]{:S(2)}) %all-to-all-start) | async-done | bytes 262176 | tf_op jit(solution)/shard_map/all_to_all | solution.py:266
  31.4 5.6 %spectra.1 = f32[1152,128]{1,0:T(8,128)S(1)} custom-call(f32[16,32,128]{2,1,0:T(8,128)S(1)} %all-to-all-done.maps_ref, s32[1,128]{1,0:T(1,128)S(1)} %reshape.24.key_ref, bf16[6,6,96,256]{3,2,1,0:T(8,128)(2,1)S(1)} %load.1.first_ref, bf16[16,6,96,256]{3,2,1,0:T(8,128)(2,1)} %bitcast.13), custom_call_target="tpu_custom_call" | custom-call | tf_op jit(solution)/shard_map/spectra/pallas_call | solution.py:282
  37.0 24.7 %all_to_all.10 = f32[32,9,4,128]{3,2,1,0:T(4,128)S(1)} all-to-all(f32[32,9,4,128]{3,2,1,0:T(4,128)S(1)} %bitcast.11), channel_id=1, replica_groups=mesh['site'=16,'fault'=32] {'fault'}, dimensions={0} | all-to-all | bytes 1179648 | tf_op jit(solution)/shard_map/all_to_all | solution.py:298
  61.7 0.9 %invert.1 = f32[8,3,1,192]{3,2,1,0:T(1,128)} custom-call(f32[1152,128]{1,0:T(8,128)S(1)} %bitcast.10, f32[192,192]{1,0:T(8,128)S(1)} %maximum_multiply_fusion.table_ref), custom_call_target="tpu_custom_call" | custom-call | tf_op jit(solution)/shard_map/invert/pallas_call | solution.py:301
  (3 shorter events, 0.0 us)
Async XLA Ops:
  0.0 19.1 %copy-start.3 = (s32[16]{0:T(128)S(1)}, s32[16]{0:T(128)}, u32[]{:S(2)}) copy-start(s32[16]{0:T(128)} %param.12) | copy-start | bytes 196
  0.0 19.1 %copy-start.2 = (s32[32]{0:T(128)S(1)}, s32[32]{0:T(128)}, u32[]{:S(2)}) copy-start(s32[32]{0:T(128)} %param.13) | copy-start | bytes 388
  0.0 19.3 %copy-start = (s32[16,8]{0,1:T(8,128)S(1)}, s32[16,8]{0,1:T(8,128)}, u32[]{:S(2)}) copy-start(s32[16,8]{0,1:T(8,128)} %param.10) | copy-start | bytes 1540
  0.0 19.3 %copy-start.1 = (s32[16]{0:T(128)S(1)}, s32[16]{0:T(128)}, u32[]{:S(2)}) copy-start(s32[16]{0:T(128)} %param.11) | copy-start | bytes 196
  1.9 29.5 %all-to-all-start = ((f32[16,32,128]{2,1,0:T(8,128)}), f32[16,32,128]{2,1,0:T(8,128)S(1)}, u32[]{:S(2)}, u32[]{:S(2)}) async-start(f32[16,32,128]{2,1,0:T(8,128)} %pack.1), calls=%async_computation | async-start | bytes 524288 | tf_op jit(solution)/shard_map/all_to_all | solution.py:266

commit v5 on v4

--- a/solution.py
+++ b/solution.py
@@ -10,6 +10,7 @@
 STEP = 16
 AHEAD = 2
 EARLY = 6
+SENDS = 2
 
 
 def sin_cos(angle):
@@ -51,22 +52,24 @@
 
 def pack_kernel(slip_hbm, time_hbm, out_hbm, slip_ref, time_ref, block_ref, sems):
     copies = [
-        pltpu.make_async_copy(slip_hbm, slip_ref, sems.at[0]),
-        pltpu.make_async_copy(time_hbm, time_ref, sems.at[1]),
+        pltpu.make_async_copy(time_hbm, time_ref, sems.at[0]),
+        pltpu.make_async_copy(slip_hbm, slip_ref, sems.at[1]),
     ]
     for copy in copies:
         copy.start()
-    share = slip_ref.shape[1]
-    copies[0].wait()
-    block_ref[:share] = slip_ref[...].astype(jnp.float32).T
-    copies[1].wait()
-    block_ref[share:] = time_ref[...].T
-    sends = [
-        pltpu.make_async_copy(block_ref, out_hbm.at[peer], sems.at[2 + peer])
-        for peer in range(out_hbm.shape[0])
-    ]
-    for send in sends:
-        send.start()
+    for copy in copies:
+        copy.wait()
+    block = jnp.concatenate([slip_ref[...].astype(jnp.float32).T, time_ref[...].T], axis=0)
+    peers = out_hbm.shape[0]
+    sends = []
+    for first in range(0, peers, peers // SENDS):
+        part = pl.ds(first, peers // SENDS)
+        for peer in range(first, first + peers // SENDS):
+            block_ref[peer] = block
+        sends.append(
+            pltpu.make_async_copy(block_ref.at[part], out_hbm.at[part], sems.at[2 + len(sends)])
+        )
+        sends[-1].start()
     for send in sends:
         send.wait()
 
@@ -257,8 +260,8 @@
         scratch_shapes=[
             pltpu.VMEM((tiles * rows, share), slip_map.dtype),
             pltpu.VMEM((tiles * rows, share), rupture_time.dtype),
-            pltpu.VMEM((2 * share, tiles * rows), jnp.float32),
-            pltpu.SemaphoreType.DMA((2 + sites,)),
+            pltpu.VMEM((sites, 2 * share, tiles * rows), jnp.float32),
+            pltpu.SemaphoreType.DMA((2 + SENDS,)),
         ],
         compiler_params=pltpu.CompilerParams(vmem_limit_bytes=4 << 20),
         name="pack",

time: 63 us -> 62.8 us (level)
  no operation moved by 1% of the time
where the time goes in v5:
time: 62.8 us; the launch traced here: 62.5 us
  blocking collectives  24.7 us (39%)
  starting transfers between devices  15.7 us (25%)
  waiting for transfers between devices  11.4 us (18%)
  Pallas kernels  9.75 us (16%)
  other arithmetic  0.64 us (1%)
    all_to_all x1, blocking collectives, per_device(): lax.all_to_all(partial.reshape(ruptures, -1, rows // 2, 128), 'fault', 0,...  24.7 us
    all_to_all x1, starting transfers between devices, per_device(): maps = lax.all_to_all(packed, 'site', 0, 0, tiled=True)  15.7 us
    all_to_all x1, waiting for transfers between devices, per_device(): maps = lax.all_to_all(packed, 'site', 0, 0, tiled=True)  11.4 us
    pallas_call x1, Pallas kernels, per_device(): pl.pallas_call(main_kernel, in_specs=[vmem(), vmem(), vmem(), hbm()], out...  5.63 us
    pallas_call x1, Pallas kernels, per_device(): pl.pallas_call(pack_kernel, in_specs=[hbm(), hbm()], out_specs=hbm(), out...  1.69 us
    pallas_call x1, Pallas kernels, per_device(): pl.pallas_call(load_kernel, in_specs=[hbm()], out_specs=vmem(), out_shape...  1.49 us
  transfers between devices with their start and end apart: 1, of which 1 were waited for; matrix products, arithmetic and copies ran while one was open for 1% of the time, Pallas kernels for 2%

profile of v5, /device:TPU:1, one launch (start us, length us, event | category | flops | bytes accessed | tf_op | source)
XLA Modules:
  0.0 62.5 jit_solution(11322449329877259124)
XLA Ops:
  0.0 0.0 copy-start.3
  0.0 0.0 copy-start.2
  0.0 0.0 copy-start
  0.0 0.0 copy-start.1
  0.0 1.7 %pack.1 = f32[16,32,128]{2,1,0:T(8,128)} custom-call(bf16[128,16]{1,0:T(8,128)(2,1)} %bitcast.15, f32[128,16]{1,0:T(8,128)} %bitcast.14), custom_call_target="tpu_custom_call" | custom-call | tf_op jit(solution)/shard_map/pack/pallas_call | solution.py:255
  1.7 15.7 %all-to-all-start = ((f32[16,32,128]{2,1,0:T(8,128)}), f32[16,32,128]{2,1,0:T(8,128)S(1)}, u32[]{:S(2)}, u32[]{:S(2)}) async-start(f32[16,32,128]{2,1,0:T(8,128)} %pack.1), calls=%async_computation | async-start | bytes 524288 | tf_op jit(solution)/shard_map/all_to_all | solution.py:269
  17.5 1.5 %load.1.first_ref = bf16[6,6,96,256]{3,2,1,0:T(8,128)(2,1)S(1)} custom-call(bf16[16,6,96,256]{3,2,1,0:T(8,128)(2,1)} %bitcast.12), custom_call_target="tpu_custom_call" | custom-call | tf_op jit(solution)/shard_map/load/pallas_call | solution.py:276
  19.0 0.0 copy-done.3
  19.0 0.0 copy-done.2
  19.0 0.2 select_reduce_fusion
  19.2 0.0 copy-done
  19.2 0.0 copy-done.1
  19.2 0.1 copy.12
  19.3 0.1 reshape.24.key_ref
  19.4 0.4 sine_negate_fusion
  19.8 11.4 %all-to-all-done.maps_ref = f32[16,32,128]{2,1,0:T(8,128)S(1)} async-done(((f32[16,32,128]{2,1,0:T(8,128)}), f32[16,32,128]{2,1,0:T(8,128)S(1)}, u32[]{:S(2)}, u32[]{:S(2)}) %all-to-all-start) | async-done | bytes 262176 | tf_op jit(solution)/shard_map/all_to_all | solution.py:269
  31.2 5.6 %spectra.1 = f32[1152,128]{1,0:T(8,128)S(1)} custom-call(f32[16,32,128]{2,1,0:T(8,128)S(1)} %all-to-all-done.maps_ref, s32[1,128]{1,0:T(1,128)S(1)} %reshape.24.key_ref, bf16[6,6,96,256]{3,2,1,0:T(8,128)(2,1)S(1)} %load.1.first_ref, bf16[16,6,96,256]{3,2,1,0:T(8,128)(2,1)} %bitcast.13), custom_call_target="tpu_custom_call" | custom-call | tf_op jit(solution)/shard_map/spectra/pallas_call | solution.py:285
  36.9 24.7 %all_to_all.10 = f32[32,9,4,128]{3,2,1,0:T(4,128)S(1)} all-to-all(f32[32,9,4,128]{3,2,1,0:T(4,128)S(1)} %bitcast.11), channel_id=1, replica_groups=mesh['site'=16,'fault'=32] {'fault'}, dimensions={0} | all-to-all | bytes 1179648 | tf_op jit(solution)/shard_map/all_to_all | solution.py:301
  61.6 0.9 %invert.1 = f32[8,3,1,192]{3,2,1,0:T(1,128)} custom-call(f32[1152,128]{1,0:T(8,128)S(1)} %bitcast.10, f32[192,192]{1,0:T(8,128)S(1)} %maximum_multiply_fusion.table_ref), custom_call_target="tpu_custom_call" | custom-call | tf_op jit(solution)/shard_map/invert/pallas_call | solution.py:304
  (3 shorter events, 0.0 us)
Async XLA Ops:
  0.0 19.0 %copy-start.3 = (s32[16]{0:T(128)S(1)}, s32[16]{0:T(128)}, u32[]{:S(2)}) copy-start(s32[16]{0:T(128)} %param.12) | copy-start | bytes 196
  0.0 19.0 %copy-start.2 = (s32[32]{0:T(128)S(1)}, s32[32]{0:T(128)}, u32[]{:S(2)}) copy-start(s32[32]{0:T(128)} %param.13) | copy-start | bytes 388
  0.0 19.2 %copy-start = (s32[16,8]{0,1:T(8,128)S(1)}, s32[16,8]{0,1:T(8,128)}, u32[]{:S(2)}) copy-start(s32[16,8]{0,1:T(8,128)} %param.10) | copy-start | bytes 1540
  0.0 19.2 %copy-start.1 = (s32[16]{0:T(128)S(1)}, s32[16]{0:T(128)}, u32[]{:S(2)}) copy-start(s32[16]{0:T(128)} %param.11) | copy-start | bytes 196
  1.7 29.5 %all-to-all-start = ((f32[16,32,128]{2,1,0:T(8,128)}), f32[16,32,128]{2,1,0:T(8,128)S(1)}, u32[]{:S(2)}, u32[]{:S(2)}) async-start(f32[16,32,128]{2,1,0:T(8,128)} %pack.1), calls=%async_computation | async-start | bytes 524288 | tf_op jit(solution)/shard_map/all_to_all | solution.py:269
